TPU v7x, 32 devices: a whole 2x2x4 slice. The times are simulated.
32 devices in a mesh: groups: 2 (over x), grid: 4 (over y, core), chol: 4 (over z).
Axes of the slice: x: 2, y: 2, z: 4, core: 2. Of those that a mesh axis runs over, the one named last changes fastest.
Arguments:
- chol_block: float32 [8, 1024, 1024], P(('groups', 'chol'), 'grid'), parts along dimension 0, may hold values from -6 to 6
- orbitals: float32 [8192, 1024], P(('groups', 'grid')), parts along dimension 0, may hold values from -0.1875 to 0.1875
- fit_in: float32 [8192, 4096], P(('groups', 'chol'), 'grid'), parts along dimension 0, may hold values from -6 to 6
Outputs:
- fit_out: float32 [8192, 4096], P(('groups', 'chol'), 'grid'), parts along dimension 0
There are 2 independent parts, one for each index of `groups`. A program takes and returns all parts, laid end to end along the dimension named above; each array names one. Nothing has to cross between parts.
All inputs are finite; a program needn't handle non-finite values.
Results may differ from a plain program's by a relative error of at most 0.000096.
Values sent between devices are 32-bit elements; how exact they have to be, the bound alone decides.
A program may use at most 64 MiB of HBM per device.

v0:
```python
import jax
import jax.numpy as jnp
from jax import lax
from jax.sharding import PartitionSpec as P


def on_device(chol_block, orbitals, fit_in):
    partial_half = jnp.einsum(
        "pr,vrq->vpq",
        orbitals,
        lax.all_gather(chol_block, "grid", axis=1, tiled=True),
        precision=lax.Precision.HIGHEST,
    )
    summed = jnp.einsum("vpq,pq->vp", partial_half, orbitals, precision=lax.Precision.HIGHEST)
    contracted = jnp.transpose(summed)
    tile_rows = fit_in.shape[0]
    widened = lax.all_gather(contracted, "chol", axis=1, tiled=True)
    everyone = lax.all_gather(widened, "grid", axis=0, tiled=True)
    own_rows = lax.dynamic_slice_in_dim(everyone, lax.axis_index("chol") * tile_rows, tile_rows, 0)
    fit_tile = jnp.dot(own_rows, jnp.transpose(widened), precision=lax.Precision.HIGHEST)
    return fit_in + fit_tile


def solution(mesh):
    placed = (
        P(("groups", "chol"), "grid", None),
        P(("groups", "grid"), None),
        P(("groups", "chol"), "grid"),
    )
    return jax.shard_map(
        on_device,
        mesh=mesh,
        in_specs=placed,
        out_specs=P(("groups", "chol"), "grid"),
        check_vma=False,
    )
```

profile of v0, /device:TPU:0, one launch (start us, length us, event | category | flops | bytes accessed | tf_op | source)
XLA Modules:
  0.0 116.4 jit_solution(9180656341693434953)
XLA Ops:
  6.5 0.0 all-gather.3.cloned.1.call-start
  6.5 0.7 all-gather.3.cloned.1.call-update
  7.3 38.9 %all-gather.3.cloned.1.call-done = f32[1,1024,1024]{2,1,0:T(8,128)} async-done(((f32[1,256,1024]{2,1,0:T(8,128)}), f32[1,1024,1024]{2,1,0:T(8,128)}) %all-gather.3.cloned.1.call-update) | async-done | bytes 4194320 | tf_op jit(solution)/shard_map/all_gather | solution.py:11
  46.1 30.4 %fusion.2 = f32[1024,1024]{0,1:T(8,128)} fusion(f32[1024,1024]{1,0:T(8,128)} %param.4, f32[1,1024,1024]{2,1,0:T(8,128)} %all-gather.3.cloned.1.call-done), kind=kOutput, calls=%fused_computation.3 | convolution fusion | flops 12884901888 | bytes 12582912 | tf_op jit(solution)/shard_map/pr,vrq->vpq/dot_general | solution.py:8
  76.6 5.3 %copy.7 = f32[1024,1024]{1,0:T(8,128)} copy(f32[1024,1024]{0,1:T(8,128)} %fusion.2) | data formatting | bytes 8388608
  81.9 0.0 copy-start
  81.9 4.0 %multiply_reduce_fusion = f32[1024]{0:T(1024)S(1)} fusion(f32[1024,1024]{1,0:T(8,128)} %copy.7, f32[1024,1024]{1,0:T(8,128)} %param.4), kind=kLoop, calls=%fused_computation.2 | loop fusion | flops 2096128 | bytes 8392704 | tf_op jit(solution)/shard_map/vpq,pq->vp/dot_general | solution.py:14
  86.0 13.2 %all-gather = f32[4,1,1024]{2,1,0:T(1,128)S(1)} all-gather(f32[1,1,1024]{2,1,0:T(1,128)S(1)} %bitcast.21), channel_id=1, replica_groups=mesh['groups'=2,'grid'=4,'chol'=4] {'chol'}, dimensions={0}, use_global_device_ids=true | all-gather | bytes 20480 | tf_op jit(solution)/shard_map/all_gather | solution.py:17
  99.1 5.2 %all_gather.11 = f32[4096,4]{0,1:T(4,128)S(1)} all-gather(f32[1024,4]{0,1:T(4,128)S(1)} %bitcast.20), channel_id=1, replica_groups=mesh['groups'=2,'grid'=4,'chol'=4] {'grid'}, dimensions={0}, use_global_device_ids=true | all-gather | bytes 81920 | tf_op jit(solution)/shard_map/all_gather | solution.py:18
  104.4 0.0 copy-done
  104.4 5.2 %convolution_add_fusion = f32[1024,1024]{1,0:T(8,128)} fusion(f32[1024,1024]{1,0:T(8,128)S(1)} %copy-done, f32[4096,4]{0,1:T(4,128)S(1)} %all_gather.11, s32[]{:T(128)S(6)} %select_n.3, f32[4,1,1024]{2,1,0:T(1,128)S(1)} %all-gather), kind=kOutput, calls=%fused_computation.4 | convolution fusion | flops 51380224 | bytes 8421380 | tf_op jit(solution)/shard_map/dot_general | solution.py:20
  (1 shorter events, 0.0 us)
Async XLA Ops:
  6.5 39.6 %all-gather.3.cloned.1.call-start = ((), (), s32[]{:S(2)}) async-start(), calls=%async_computation | async-start | bytes 5242880 | tf_op jit(solution)/shard_map/all_gather | solution.py:11
  81.9 22.5 %copy-start = (f32[1024,1024]{1,0:T(8,128)S(1)}, f32[1024,1024]{1,0:T(8,128)}, u32[]{:S(2)}) copy-start(f32[1024,1024]{1,0:T(8,128)} %param.5) | copy-start | bytes 12582916
Sparse Core Ops, SparseCore 0:
  8.9 37.1 all-gather.2
where the time goes:
time: 117 us; the launch traced here: 116 us
  waiting for transfers between devices  39.6 us (34%)
  matrix products  35.6 us (30%)
  blocking collectives  18.4 us (16%)
  between operations  13.4 us (11%)
  local copies, waits for them, and re-layouts  5.36 us (5%)
  other arithmetic  4.04 us (3%)
    all_gather x1, waiting for transfers between devices, on_device(): lax.all_gather(chol_block, 'grid', axis=1, tiled=True)  38.9 us
    dot_general x1, matrix products, on_device(): jnp.einsum('pr,vrq->vpq', orbitals, lax.all_gather(chol_block, 'grid', ax...  30.4 us
    all_gather x1, blocking collectives, on_device(): widened = lax.all_gather(contracted, 'chol', axis=1, tiled=True)  13.2 us
    unnamed x4, local copies, waits for them, and re-layouts  5.36 us
    all_gather x1, blocking collectives, on_device(): everyone = lax.all_gather(widened, 'grid', axis=0, tiled=True)  5.23 us
    dot_general x1, matrix products, on_device(): jnp.dot(own_rows, jnp.transpose(widened), precision=lax.Precision.HIGHEST)  5.2 us
    dot_general x1, other arithmetic, on_device(): jnp.einsum('vpq,pq->vp', partial_half, orbitals, precision=lax.Precision....  4.04 us
  transfers between devices with their start and end apart: 1, of which 1 were waited for; matrix products, arithmetic and copies ran while one was open for 0% of the time, Pallas kernels for 0%

commit v1 on v0

--- a/solution.py
+++ b/solution.py
@@ -14,7 +14,12 @@
     summed = jnp.einsum("vpq,pq->vp", partial_half, orbitals, precision=lax.Precision.HIGHEST)
     contracted = jnp.transpose(summed)
     tile_rows = fit_in.shape[0]
-    widened = lax.all_gather(contracted, "chol", axis=1, tiled=True)
+    ring = [contracted]
+    for hop in range(3):
+        ring.append(lax.ppermute(ring[-1], "chol", [(dev, (dev + 1) % 4) for dev in range(4)]))
+    widened = jnp.roll(
+        jnp.concatenate(ring[::-1], axis=1), (lax.axis_index("chol") + 1) * ring[0].shape[1], axis=1
+    )
     everyone = lax.all_gather(widened, "grid", axis=0, tiled=True)
     own_rows = lax.dynamic_slice_in_dim(everyone, lax.axis_index("chol") * tile_rows, tile_rows, 0)
     fit_tile = jnp.dot(own_rows, jnp.transpose(widened), precision=lax.Precision.HIGHEST)

time: 117 us -> 121 us (1.034)
  waiting for transfers between devices: 39.6 us -> 54.3 us
  blocking collectives: 18.4 us -> 5.25 us
  starting transfers between devices: 0.01 us -> 1.55 us
  matrix products: 35.6 us -> 37.1 us
    ppermute x0 -> x3, waiting for transfers between devices: none -> 14.7 us  [on_device(): lax.ppermute(ring[-1], 'chol', [(dev, (dev + 1) % 4) for dev in range(4)])]
    all_gather x1 -> x0, blocking collectives: 13.2 us -> none  [on_device(): widened = lax.all_gather(contracted, 'chol', axis=1, tiled=True)]
    ppermute x0 -> x3, starting transfers between devices: none -> 1.54 us  [on_device(): lax.ppermute(ring[-1], 'chol', [(dev, (dev + 1) % 4) for dev in range(4)])]
    dot_general x1, matrix products: 5.2 us -> 6.65 us  [on_device(): jnp.dot(own_rows, jnp.transpose(widened), precision=lax.Precision.HIGHEST)]
    unnamed x4 -> x1, local copies, waits for them, and re-layouts: 5.36 us -> 5.36 us
  transfers between devices with their start and end apart: 1 -> 4, of which waited for: 1 -> 4; matrix products, arithmetic and copies ran while one was open for 0% -> 0% of each run, Pallas kernels for 0% -> 0%
where the time goes in v1:
time: 121 us
  waiting for transfers between devices  54.3 us (45%)
  matrix products  37.1 us (31%)
  between operations  13.4 us (11%)
  local copies, waits for them, and re-layouts  5.43 us (4%)
  blocking collectives  5.25 us (4%)
  other arithmetic  3.91 us (3%)
  starting transfers between devices  1.55 us (1%)
    all_gather x1, waiting for transfers between devices, on_device(): lax.all_gather(chol_block, 'grid', axis=1, tiled=True)  38.9 us
    dot_general x1, matrix products, on_device(): jnp.einsum('pr,vrq->vpq', orbitals, lax.all_gather(chol_block, 'grid', ax...  30.4 us
    ppermute x3, waiting for transfers between devices, on_device(): lax.ppermute(ring[-1], 'chol', [(dev, (dev + 1) % 4) for dev in range(4)])  14.7 us
    dot_general x1, matrix products, on_device(): jnp.dot(own_rows, jnp.transpose(widened), precision=lax.Precision.HIGHEST)  6.65 us
    unnamed x1, local copies, waits for them, and re-layouts  5.36 us
    all_gather x1, blocking collectives, on_device(): everyone = lax.all_gather(widened, 'grid', axis=0, tiled=True)  5.25 us
    dot_general x1, other arithmetic, on_device(): jnp.einsum('vpq,pq->vp', partial_half, orbitals, precision=lax.Precision....  3.91 us
  transfers between devices with their start and end apart: 4, of which 4 were waited for; matrix products, arithmetic and copies ran while one was open for 0% of the time, Pallas kernels for 0%

profile of v1, /device:TPU:0, one launch (start us, length us, event | category | flops | bytes accessed | tf_op | source)
XLA Modules:
  0.0 120.9 jit_solution(9753893857522336005)
XLA Ops:
  6.5 0.0 all-gather.2.cloned.1.call-start
  6.5 0.7 all-gather.2.cloned.1.call-update
  7.3 38.9 %all-gather.2.cloned.1.call-done = f32[1,1024,1024]{2,1,0:T(8,128)} async-done(((f32[1,256,1024]{2,1,0:T(8,128)}), f32[1,1024,1024]{2,1,0:T(8,128)}) %all-gather.2.cloned.1.call-update) | async-done | bytes 4194320 | tf_op jit(solution)/shard_map/all_gather | solution.py:11
  46.1 30.4 %fusion.2 = f32[1024,1024]{0,1:T(8,128)} fusion(f32[1024,1024]{1,0:T(8,128)} %param.4, f32[1,1024,1024]{2,1,0:T(8,128)} %all-gather.2.cloned.1.call-done), kind=kOutput, calls=%fused_computation.3 | convolution fusion | flops 12884901888 | bytes 12582912 | tf_op jit(solution)/shard_map/pr,vrq->vpq/dot_general | solution.py:8
  76.6 5.4 %copy.7 = f32[1024,1024]{1,0:T(8,128)} copy(f32[1024,1024]{0,1:T(8,128)} %fusion.2) | data formatting | bytes 8388608
  81.9 3.9 %multiply_reduce_fusion = f32[1024]{0:T(1024)S(1)} fusion(f32[1024,1024]{1,0:T(8,128)} %copy.7, f32[1024,1024]{1,0:T(8,128)} %param.4), kind=kLoop, calls=%fused_computation.2 | loop fusion | flops 2096128 | bytes 8392704 | tf_op jit(solution)/shard_map/vpq,pq->vp/dot_general | solution.py:14
  85.8 1.5 %collective-permute-start = (f32[1024,1]{0,1:T(1,128)S(1)}, f32[1024,1]{0,1:T(1,128)S(1)}, u32[]{:S(2)}, u32[]{:S(2)}) collective-permute-start(f32[1024,1]{0,1:T(1,128)S(1)} %bitcast.14), channel_id=1, source_target_pairs={{0,1},{1,2},{2,3},{3,0},{4,5},{5,6},{6,7},{7,4},{8,9},{9,10},{10,1... | collective-permute-start | bytes 12296 | tf_op jit(solution)/shard_map/ppermute | solution.py:19
  87.4 3.9 %collective-permute-done = f32[1024,1]{0,1:T(1,128)S(1)} collective-permute-done((f32[1024,1]{0,1:T(1,128)S(1)}, f32[1024,1]{0,1:T(1,128)S(1)}, u32[]{:S(2)}, u32[]{:S(2)}) %collective-permute-start) | collective-permute-done | bytes 4128 | tf_op jit(solution)/shard_map/ppermute | solution.py:19
  91.3 0.0 collective-permute-start.1
  91.3 5.4 %collective-permute-done.1 = f32[1024,1]{0,1:T(1,128)S(1)} collective-permute-done((f32[1024,1]{0,1:T(1,128)S(1)}, f32[1024,1]{0,1:T(1,128)S(1)}, u32[]{:S(2)}, u32[]{:S(2)}) %collective-permute-start.1) | collective-permute-done | bytes 4128 | tf_op jit(solution)/shard_map/ppermute | solution.py:19
  96.7 0.0 collective-permute-start.2
  96.7 5.4 %collective-permute-done.2 = f32[1024,1]{0,1:T(1,128)S(1)} collective-permute-done((f32[1024,1]{0,1:T(1,128)S(1)}, f32[1024,1]{0,1:T(1,128)S(1)}, u32[]{:S(2)}, u32[]{:S(2)}) %collective-permute-start.2) | collective-permute-done | bytes 4128 | tf_op jit(solution)/shard_map/ppermute | solution.py:19
  102.1 0.1 concatenate.6
  102.2 5.2 %all_gather.7 = f32[4096,4]{0,1:T(4,128)S(1)} all-gather(f32[1024,4]{0,1:T(4,128)S(1)} %constant_dynamic-slice_fusion), channel_id=1, replica_groups=mesh['groups'=2,'grid'=4,'chol'=4] {'grid'}, dimensions={0}, use_global_device_ids=true | all-gather | bytes 81920 | tf_op jit(solution)/shard_map/all_gather | solution.py:23
  107.4 6.6 %convolution_add_fusion = f32[1024,1024]{1,0:T(8,128)} fusion(f32[1024,1024]{1,0:T(8,128)} %param.5, f32[1024,4]{0,1:T(4,128)S(1)} %constant_dynamic-slice_fusion, f32[4096,4]{0,1:T(4,128)S(1)} %all_gather.7, s32[]{:T(128)S(6)} %select_n.18), kind=kOutput, calls=%fused_computation.4 | convolution fusion | flops 51380224 | bytes 8421380 | tf_op jit(solution)/shard_map/dot_general | solution.py:25
  (1 shorter events, 0.0 us)
Async XLA Ops:
  6.5 39.6 %all-gather.2.cloned.1.call-start = ((), (), s32[]{:S(2)}) async-start(), calls=%async_computation | async-start | bytes 5242880 | tf_op jit(solution)/shard_map/all_gather | solution.py:11
  85.8 5.5 %collective-permute-start = (f32[1024,1]{0,1:T(1,128)S(1)}, f32[1024,1]{0,1:T(1,128)S(1)}, u32[]{:S(2)}, u32[]{:S(2)}) collective-permute-start(f32[1024,1]{0,1:T(1,128)S(1)} %bitcast.14), channel_id=1, source_target_pairs={{0,1},{1,2},{2,3},{3,0},{4,5},{5,6},{6,7},{7,4},{8,9},{9,10},{10,1... | collective-permute-start | bytes 12296 | tf_op jit(solution)/shard_map/ppermute | solution.py:19
  91.3 5.4 %collective-permute-start.1 = (f32[1024,1]{0,1:T(1,128)S(1)}, f32[1024,1]{0,1:T(1,128)S(1)}, u32[]{:S(2)}, u32[]{:S(2)}) collective-permute-start(f32[1024,1]{0,1:T(1,128)S(1)} %collective-permute-done), channel_id=1, source_target_pairs={{0,1},{1,2},{2,3},{3,0},{4,5},{5,6},{6,7},{7,4},{8,9},{9,10},{10,1... | collective-permute-start | bytes 12296 | tf_op jit(solution)/shard_map/ppermute | solution.py:19
  96.7 5.4 %collective-permute-start.2 = (f32[1024,1]{0,1:T(1,128)S(1)}, f32[1024,1]{0,1:T(1,128)S(1)}, u32[]{:S(2)}, u32[]{:S(2)}) collective-permute-start(f32[1024,1]{0,1:T(1,128)S(1)} %collective-permute-done.1), channel_id=1, source_target_pairs={{0,1},{1,2},{2,3},{3,0},{4,5},{5,6},{6,7},{7,4},{8,9},{9,10},{10,1... | collective-permute-start | bytes 12296 | tf_op jit(solution)/shard_map/ppermute | solution.py:19
Sparse Core Ops, SparseCore 0:
  8.9 37.1 all-gather.1
